TPU v7x, 32 devices: a whole 2x2x4 slice. The times are simulated.
32 devices in a mesh: row: 4 (over y, x), col: 8 (over z, core).
Axes of the slice: x: 2, y: 2, z: 4, core: 2. Of those that a mesh axis runs over, the one named last changes fastest.
Arguments:
- coupling: float32 [4, 4608, 18432], P(None, 'col', 'row'), may hold values from -0.046875 to 0.046875
- energies: float32 [18432], P(('row', 'col')), may hold values from 0.7 to 14.2
- block: float32 [18432, 16], P(('row', 'col')), may hold values from -6 to 6
Outputs:
- basis: float32 [18432, 16], P(('row', 'col'))
- projections: float32 [2, 16, 16], replicated
- factors: float32 [2, 16, 16], replicated
All inputs are finite; a program needn't handle non-finite values.
Results may differ from a plain program's by a relative error of at most 0.0003.
Values sent between devices are 32-bit elements; how exact they have to be, the bound alone decides.
No kernel may reach another device: no remote copies, remote signals or barrier semaphores. Data moves between devices by JAX's collectives and lax.ppermute only.
A program may use at most 128 MiB of HBM per device.

v0:
```python
import jax
import jax.numpy as jnp
from jax import lax
from jax.sharding import PartitionSpec as P

N = 18432
ITERS = 2
precise = lax.Precision.HIGHEST


def combined(moments_local):
    return lax.psum(moments_local, "row")


def on_device(coupling, energies, block):
    segment = block.shape[0]
    width = block.shape[1]
    column = lax.axis_index("col")
    current, energy_rows = (
        lax.all_gather(block, "col", axis=0, tiled=True),
        lax.all_gather(energies, "col", axis=0, tiled=True),
    )
    prior = jnp.zeros_like(current)
    projection_list = []
    factor_list = []
    for section in range(ITERS):
        own_rows = lax.dynamic_slice_in_dim(current, column * segment, segment, 0)
        column_block = current
        spread = lax.all_gather(own_rows, "row", axis=0, tiled=True)
        spread = spread.reshape(coupling.shape[0], segment, width)
        direct = lax.psum_scatter(
            jnp.einsum("aig,gk->aik", coupling, column_block, precision=precise),
            "row",
            scatter_dimension=0,
            tiled=True,
        ).reshape(segment, width)
        partial_value = jnp.einsum("aig,aik->gk", coupling, spread, precision=precise)
        transposed = lax.psum(partial_value, "col")
        direct_rows = lax.all_gather(direct, "col", axis=0, tiled=True)
        product = energy_rows[:, None] * current + direct_rows + transposed
        stacked = jnp.concatenate([current, prior, product], axis=1)
        moments = combined(jnp.einsum("nk,nl->kl", stacked, stacked, precision=precise)) / N
        projection = moments[:width, 2 * width :]
        cross = moments[width : 2 * width, 2 * width :]
        weights = jnp.concatenate([-projection, -cross, jnp.eye(width, dtype=jnp.float32)], axis=0)
        gram_matrix = jnp.dot(
            weights.T, jnp.dot(moments, weights, precision=precise), precision=precise
        )
        factor = jnp.linalg.cholesky(gram_matrix)
        residual = (
            product
            - jnp.dot(current, projection, precision=precise)
            - jnp.dot(prior, cross, precision=precise)
        )
        prior = current
        current = jax.scipy.linalg.solve_triangular(factor, residual.T, lower=True).T
        projection_list.append(projection)
        factor_list.append(factor)
    basis = lax.dynamic_slice_in_dim(current, column * segment, segment, 0)
    return (basis, jnp.stack(projection_list), jnp.stack(factor_list))


def solution(mesh):
    placed = (P(None, "col", "row"), P(("row", "col")), P(("row", "col"), None))
    return jax.shard_map(
        on_device,
        mesh=mesh,
        in_specs=placed,
        out_specs=(P(("row", "col"), None), P(), P()),
        check_vma=False,
    )
```

profile of v0, /device:TPU:0, one launch (start us, length us, event | category | flops | bytes accessed | tf_op | source)
XLA Modules:
  0.0 340.6 jit_solution(8555709565530399333)
XLA Ops:
  8.0 0.0 reduce-scatter.7.cloned.1.call-start
  8.0 16.3 %all-gather.2 = f32[8,576,16]{1,2,0:T(8,128)S(1)} all-gather(f32[1,576,16]{1,2,0:T(8,128)} %bitcast.93), channel_id=1, replica_groups=mesh['row'=4,'col'=8] {'col'}, dimensions={0}, use_global_device_ids=true | all-gather | bytes 331776 | tf_op jit(solution)/shard_map/all_gather | solution.py:20
  24.3 0.1 copy.9
  24.4 0.1 reshape.46
  24.6 40.0 %fusion.44 = f32[4,576,16]{1,2,0:T(8,128)} fusion(f32[4,576,4608]{2,1,0:T(8,128)} %param.6, f32[4608,16,1]{0,1,2:T(8,128)S(1)} %reshape.46), kind=kOutput, calls=%fused_computation.77 | convolution fusion | flops 2038431744 | bytes 42909696 | tf_op jit(solution)/shard_map/aig,gk->aik/dot_general | solution.py:32
  64.6 0.0 all-reduce.6.cloned.1.call-start
  64.7 0.1 reshape.37
  64.8 0.1 dynamic-slice_bitcast_fusion.2
  64.9 8.8 %all-gather.3 = f32[4,576,16]{1,2,0:T(8,128)S(1)} all-gather(f32[1,576,16]{1,2,0:T(8,128)S(1)} %dynamic-slice_bitcast_fusion.2), channel_id=1, replica_groups=mesh['row'=4,'col'=8] {'row'}, dimensions={0}, use_global_device_ids=true | all-gather | bytes 184320 | tf_op jit(solution)/shard_map/all_gather | solution.py:29
  73.6 24.6 %convolution_bitcast_fusion.3 = f32[4608,16]{0,1:T(8,128)} fusion(f32[4,576,16]{1,2,0:T(8,128)S(1)} %all-gather.3, f32[4,576,4608]{2,1,0:T(8,128)} %param.6), kind=kOutput, calls=%fused_computation.9 | convolution fusion | flops 2038431744 | bytes 42909696 | tf_op jit(solution)/shard_map/aig,aik->gk/dot_general | solution.py:37
  98.3 0.0 reduce-scatter.9.cloned.1.call-start
  98.3 0.6 dynamic-slice.8
  99.6 0.1 pad.14.clone
  99.7 0.3 dynamic-update-slice.2
  99.9 27.3 %all-reduce = f32[4608]{0:T(1024)S(1)} all-reduce(f32[4608]{0:T(1024)S(1)} %dynamic-update-slice.2), channel_id=1, replica_groups=mesh['row'=4,'col'=8] {'col'}, use_global_device_ids=true, to_apply=%add | all-reduce | flops 4608 | bytes 36864
  127.2 0.9 copy.10
  128.2 24.6 %all-gather = f32[1,4608,16]{2,0,1:T(1,128)S(1)} all-gather(f32[1,576,16]{2,0,1:T(1,128)S(1)} %copy.10), channel_id=2, replica_groups=mesh['row'=4,'col'=8] {'col'}, dimensions={1}, use_global_device_ids=true | all-gather | bytes 331776 | tf_op jit(solution)/shard_map/all_gather | solution.py:39
  152.7 2.2 copy.11
  154.9 0.0 all-reduce.6.cloned.1.call-done
  154.9 1.0 fusion.19
  156.0 0.9 fusion.5
  156.9 15.3 %psum.29 = f32[48,48]{1,0:T(8,128)S(1)} all-reduce(f32[48,48]{1,0:T(8,128)S(1)} %fusion.5), channel_id=1, replica_groups=mesh['row'=4,'col'=8] {'row'}, use_global_device_ids=true, to_apply=%region_2.0 | all-reduce | flops 2304 | bytes 18432 | tf_op jit(solution)/shard_map/psum | solution.py:12
  172.3 0.7 slice_bitcast_fusion.1
  172.9 0.1 copy.12
  173.0 0.1 copy.13
  173.1 0.2 fusion.40
  173.3 0.2 fusion.43
  173.5 0.1 copy.14
  173.6 1.5 cholesky.44
  175.1 0.6 compare_reduce_fusion.1
  175.7 0.6 fusion.37
  176.4 1.2 custom-call.6
  177.6 0.5 fusion.4
  178.2 0.4 fusion.23
  178.6 39.3 %convolution_bitcast_fusion.4 = f32[4,576,16]{1,2,0:T(8,128)} fusion(f32[4,576,4608]{2,1,0:T(8,128)} %param.6, f32[16,4608]{1,0:T(8,128)S(1)} %fusion.23), kind=kOutput, calls=%fused_computation.10 | convolution fusion | flops 2038431744 | bytes 42909696 | tf_op jit(solution)/shard_map/aig,gk->aik/dot_general | solution.py:32
  217.9 0.1 dynamic-slice_bitcast_fusion.1
  218.0 0.0 reduce-scatter.9.cloned.1.call-update
  218.0 0.0 all-reduce.8.cloned.1.call-start
  218.1 8.7 %all-gather.4 = f32[4,576,16]{1,2,0:T(8,128)S(1)} all-gather(f32[1,576,16]{1,2,0:T(8,128)S(1)} %dynamic-slice_bitcast_fusion.1), channel_id=1, replica_groups=mesh['row'=4,'col'=8] {'row'}, dimensions={0}, use_global_device_ids=true | all-gather | bytes 184320 | tf_op jit(solution)/shard_map/all_gather | solution.py:29
  226.8 24.6 %convolution_bitcast_fusion.2 = f32[4608,16]{0,1:T(8,128)} fusion(f32[4,576,16]{1,2,0:T(8,128)S(1)} %all-gather.4, f32[4,576,4608]{2,1,0:T(8,128)} %param.6), kind=kOutput, calls=%fused_computation.8 | convolution fusion | flops 2038431744 | bytes 42909696 | tf_op jit(solution)/shard_map/aig,aik->gk/dot_general | solution.py:37
  251.4 0.0 all-reduce.8.cloned.1.call-update
  251.4 0.0 reduce-scatter.9.cloned.1.call-done
  251.4 0.9 copy.15
  252.4 28.0 %all-gather.1 = f32[1,4608,16]{2,0,1:T(1,128)S(1)} all-gather(f32[1,576,16]{2,0,1:T(1,128)S(1)} %copy.15), channel_id=3, replica_groups=mesh['row'=4,'col'=8] {'col'}, dimensions={1}, use_global_device_ids=true | all-gather | bytes 331776 | tf_op jit(solution)/shard_map/all_gather | solution.py:39
  280.4 2.2 copy.16
  282.6 24.1 %all-reduce.8.cloned.1.call-done = f32[4608,16]{0,1:T(8,128)} async-done(((f32[4608,16]{0,1:T(8,128)}), f32[4608,16]{0,1:T(8,128)}) %all-reduce.8.cloned.1.call-update) | async-done | bytes 294928 | tf_op jit(solution)/shard_map/psum | solution.py:38
  306.7 1.1 fusion.17
  307.7 0.8 fusion.10
  308.6 16.3 %psum.31 = f32[48,48]{1,0:T(8,128)S(1)} all-reduce(f32[48,48]{1,0:T(8,128)S(1)} %fusion.10), channel_id=1, replica_groups=mesh['row'=4,'col'=8] {'row'}, use_global_device_ids=true, to_apply=%region_8.11 | all-reduce | flops 2304 | bytes 18432 | tf_op jit(solution)/shard_map/psum | solution.py:12
  324.9 0.1 slice_bitcast_fusion
  324.9 0.5 convolution_bitcast_fusion
  325.5 0.1 copy.17
  325.5 0.1 copy.18
  325.6 0.2 fusion.41
  325.8 0.2 fusion.42
  326.0 0.1 copy.19
  326.1 1.5 cholesky.55
  327.6 0.6 compare_reduce_fusion
  328.3 0.6 fusion.36
  328.9 1.2 custom-call.7
  330.1 0.5 fusion.1
  330.7 0.4 fusion.20
  331.1 0.7 dynamic-slice_bitcast_fusion
  331.8 1.3 pad_maximum_fusion
  (18 shorter events, 0.2 us)
Async XLA Ops:
  8.0 119.2 %reduce-scatter.7.cloned.1.call-start = ((), (), s32[]{:S(2)}) async-start(), calls=%async_computation.4 | async-start | bytes 204800
  24.5 73.8 %copy-start.2 = (u32[32]{0:T(128)S(1)}, u32[32]{0:T(128)}, u32[]{:S(2)}) copy-start(u32[32]{0:T(128)} %constant.50) | copy-start | bytes 388
  24.5 75.1 %copy-start.1 = (f32[576]{0:T(1024)S(1)}, f32[576]{0:T(1024)}, u32[]{:S(2)}) copy-start(f32[576]{0:T(1024)} %param.7) | copy-start | bytes 6916
  64.6 90.3 %all-reduce.6.cloned.1.call-start = ((), (), s32[]{:S(2)}) async-start(), calls=%async_computation.2 | async-start | bytes 589824 | tf_op jit(solution)/shard_map/psum | solution.py:38
  98.3 153.2 %reduce-scatter.9.cloned.1.call-start = ((), (), s32[]{:S(2)}) async-start(), calls=%async_computation.5 | async-start | bytes 204800
  127.2 124.2 %copy-start = (f32[4608]{0:T(1024)}, f32[4608]{0:T(1024)S(1)}, u32[]{:S(2)}) copy-start(f32[4608]{0:T(1024)S(1)} %all-reduce) | copy-start | bytes 55300
  218.0 88.7 %all-reduce.8.cloned.1.call-start = ((), (), s32[]{:S(2)}) async-start(), calls=%async_computation.3 | async-start | bytes 589824 | tf_op jit(solution)/shard_map/psum | solution.py:38
Sparse Core Ops, SparseCore 0:
  64.7 25.2 reduce-scatter.6
  218.1 24.4 reduce-scatter.8
Sparse Core Ops, SparseCore 1:
  98.3 55.3 all-reduce.5
  251.5 55.1 all-reduce.7
where the time goes:
time: 341 us
  blocking collectives  145 us (43%)
  matrix products  134 us (39%)
  waiting for transfers between devices  24.2 us (7%)
  between operations  16.4 us (5%)
  other arithmetic  12.2 us (4%)
  local copies, waits for them, and re-layouts  8.71 us (3%)
    dot_general x2, matrix products, on_device(): jnp.einsum('aig,gk->aik', coupling, column_block, precision=precise)  79.3 us
    all_gather x2, blocking collectives, on_device(): direct_rows = lax.all_gather(direct, 'col', axis=0, tiled=True)  52.6 us
    dot_general x2, matrix products, on_device(): jnp.einsum('aig,aik->gk', coupling, spread, precision=precise)  49.2 us
    psum x2, blocking collectives, combined(): return lax.psum(moments_local, 'row')  31.6 us
    unnamed x1, blocking collectives  27.3 us
    psum x2, waiting for transfers between devices, on_device(): transposed = lax.psum(partial_value, 'col')  24.1 us
    all_gather x2, blocking collectives, on_device(): spread = lax.all_gather(own_rows, 'row', axis=0, tiled=True)  17.5 us
    all_gather x1, blocking collectives, on_device(): lax.all_gather(block, 'col', axis=0, tiled=True)  16.3 us
  transfers between devices with their start and end apart: 4, of which 1 were waited for; matrix products, arithmetic and copies ran while one was open for 17% of the time, Pallas kernels for 0%

commit v1 on v0

--- a/solution.py
+++ b/solution.py
@@ -6,6 +6,28 @@
 N = 18432
 ITERS = 2
 precise = lax.Precision.HIGHEST
+
+
+def laid_out(parts, dim):
+    parts = jnp.moveaxis(parts, 0, dim)
+    shape = parts.shape
+    return parts.reshape(*shape[:dim], shape[dim] * shape[dim + 1], *shape[dim + 2 :])
+
+
+def doubled(x, axis):
+    count = lax.axis_size(axis)
+    tiles = x[None]
+    for level in range(count.bit_length() - 1):
+        bit = 1 << level
+        other = lax.ppermute(tiles, axis, [(i, i ^ bit) for i in range(count)])
+        both = jnp.stack([tiles, other])
+        upper = lax.axis_index(axis) >> level & 1
+        tiles = jnp.where(upper == 0, both, both[::-1]).reshape(-1, *x.shape)
+    return tiles
+
+
+def gather_by_bits(value, axis, dim):
+    return laid_out(doubled(value, axis), dim)
 
 
 def combined(moments_local):
@@ -36,7 +58,7 @@
         ).reshape(segment, width)
         partial_value = jnp.einsum("aig,aik->gk", coupling, spread, precision=precise)
         transposed = lax.psum(partial_value, "col")
-        direct_rows = lax.all_gather(direct, "col", axis=0, tiled=True)
+        direct_rows = gather_by_bits(direct, "col", 0)
         product = energy_rows[:, None] * current + direct_rows + transposed
         stacked = jnp.concatenate([current, prior, product], axis=1)
         moments = combined(jnp.einsum("nk,nl->kl", stacked, stacked, precision=precise)) / N

time: 341 us -> 391 us (1.15)
  waiting for transfers between devices: 24.2 us -> 124 us
  blocking collectives: 145 us -> 92.3 us
  starting transfers between devices: 0.17 us -> 8.23 us
  local copies, waits for them, and re-layouts: 8.71 us -> 3.26 us
    all_gather x2 -> x0, blocking collectives: 52.6 us -> none  [on_device(): direct_rows = lax.all_gather(direct, 'col', axis=0, tiled=True)]
    unnamed x6, waiting for transfers between devices: 0.09 us -> 49.4 us
    psum x2, waiting for transfers between devices: 24.1 us -> 72.2 us  [on_device(): transposed = lax.psum(partial_value, 'col')]
    ppermute x0 -> x6, starting transfers between devices: none -> 8.06 us  [doubled(): other = lax.ppermute(tiles, axis, [(i, i ^ bit) for i in range(count)])]
    all_gather x2 -> x0, local copies, waits for them, and re-layouts: 4.31 us -> none  [on_device(): direct_rows = lax.all_gather(direct, 'col', axis=0, tiled=True)]
  transfers between devices with their start and end apart: 4 -> 10, of which waited for: 1 -> 6; matrix products, arithmetic and copies ran while one was open for 17% -> 13% of each run, Pallas kernels for 0% -> 0%
where the time goes in v1:
time: 391 us
  matrix products  133 us (34%)
  waiting for transfers between devices  124 us (32%)
  blocking collectives  92.3 us (24%)
  between operations  16.5 us (4%)
  other arithmetic  12.8 us (3%)
  starting transfers between devices  8.23 us (2%)
    dot_general x2, matrix products, on_device(): jnp.einsum('aig,gk->aik', coupling, column_block, precision=precise)  79.3 us
    psum x2, waiting for transfers between devices, on_device(): transposed = lax.psum(partial_value, 'col')  72.2 us
    unnamed x6, waiting for transfers between devices  49.4 us
    dot_general x2, matrix products, on_device(): jnp.einsum('aig,aik->gk', coupling, spread, precision=precise)  49 us
    psum x2, blocking collectives, combined(): return lax.psum(moments_local, 'row')  32.5 us
    unnamed x1, blocking collectives  26 us
    all_gather x2, blocking collectives, on_device(): spread = lax.all_gather(own_rows, 'row', axis=0, tiled=True)  17.5 us
    all_gather x1, blocking collectives, on_device(): lax.all_gather(block, 'col', axis=0, tiled=True)  16.3 us
  transfers between devices with their start and end apart: 10, of which 6 were waited for; matrix products, arithmetic and copies ran while one was open for 13% of the time, Pallas kernels for 0%

profile of v1, /device:TPU:0, one launch (start us, length us, event | category | flops | bytes accessed | tf_op | source)
XLA Modules:
  0.0 390.9 jit_solution(5968175040865043137)
XLA Ops:
  8.0 16.3 %all-gather = f32[8,576,16]{1,2,0:T(8,128)S(1)} all-gather(f32[1,576,16]{1,2,0:T(8,128)} %bitcast.127), channel_id=1, replica_groups=mesh['row'=4,'col'=8] {'col'}, dimensions={0}, use_global_device_ids=true | all-gather | bytes 331776 | tf_op jit(solution)/shard_map/all_gather | solution.py:42
  24.3 0.1 copy.15
  24.4 0.1 reshape.52
  24.6 40.0 %fusion.46 = f32[4,576,16]{1,2,0:T(8,128)} fusion(f32[4,576,4608]{2,1,0:T(8,128)} %param.6, f32[4608,16,1]{0,1,2:T(8,128)S(1)} %reshape.52), kind=kOutput, calls=%fused_computation.91 | convolution fusion | flops 2038431744 | bytes 42909696 | tf_op jit(solution)/shard_map/aig,gk->aik/dot_general | solution.py:54
  64.7 25.4 %reduce-scatter.7.cloned.1.call-done = f32[1,576,16]{1,2,0:T(8,128)} async-done(((f32[4,576,16]{1,2,0:T(8,128)}), f32[1,576,16]{1,2,0:T(8,128)}) %reduce-scatter.7.cloned.1.call-update) | async-done | bytes 36880
  90.1 0.1 reshape.43
  90.2 1.3 collective-permute-done
  91.5 0.8 pad_maximum_fusion.4
  92.3 1.6 collective-permute-start.1
  93.9 0.1 dynamic-slice_bitcast_fusion.2
  93.9 8.7 %all-gather.1 = f32[4,576,16]{1,2,0:T(8,128)S(1)} all-gather(f32[1,576,16]{1,2,0:T(8,128)S(1)} %dynamic-slice_bitcast_fusion.2), channel_id=1, replica_groups=mesh['row'=4,'col'=8] {'row'}, dimensions={0}, use_global_device_ids=true | all-gather | bytes 184320 | tf_op jit(solution)/shard_map/all_gather | solution.py:51
  102.8 2.5 collective-permute-start.2
  105.2 24.5 %convolution_bitcast_fusion.3 = f32[4608,16]{0,1:T(8,128)} fusion(f32[4,576,16]{1,2,0:T(8,128)S(1)} %all-gather.1, f32[4,576,4608]{2,1,0:T(8,128)} %param.6), kind=kOutput, calls=%fused_computation.9 | convolution fusion | flops 2038431744 | bytes 42909696 | tf_op jit(solution)/shard_map/aig,aik->gk/dot_general | solution.py:59
  129.8 0.6 dynamic-slice.8
  131.1 0.1 pad.20.clone
  131.2 0.3 dynamic-update-slice.2
  131.4 26.0 %all-reduce = f32[4608]{0:T(1024)S(1)} all-reduce(f32[4608]{0:T(1024)S(1)} %dynamic-update-slice.2), channel_id=1, replica_groups=mesh['row'=4,'col'=8] {'col'}, use_global_device_ids=true, to_apply=%add | all-reduce | flops 4608 | bytes 36864
  157.6 0.1 pad_maximum_fusion
  157.7 0.2 reshape_reshape.6
  157.9 22.4 %all-reduce.6.cloned.1.call-done = f32[4608,16]{0,1:T(8,128)} async-done(((f32[4608,16]{0,1:T(8,128)}), f32[4608,16]{0,1:T(8,128)}) %all-reduce.6.cloned.1.call-update) | async-done | bytes 294928 | tf_op jit(solution)/shard_map/psum | solution.py:60
  180.3 1.0 add_add_fusion.1
  181.3 0.9 fusion.5
  182.3 16.3 %psum.29 = f32[48,48]{1,0:T(8,128)S(1)} all-reduce(f32[48,48]{1,0:T(8,128)S(1)} %fusion.5), channel_id=1, replica_groups=mesh['row'=4,'col'=8] {'row'}, use_global_device_ids=true, to_apply=%region_2.3 | all-reduce | flops 2304 | bytes 18432 | tf_op jit(solution)/shard_map/psum | solution.py:34
  198.5 0.1 slice_bitcast_fusion.1
  198.6 0.1 copy.19
  198.7 0.1 copy.20
  198.8 0.2 fusion.42
  199.0 0.2 fusion.45
  199.2 0.1 copy.21
  199.3 1.5 cholesky.44
  200.8 0.6 compare_reduce_fusion.1
  201.4 0.6 fusion.39
  202.1 1.2 custom-call.6
  203.3 0.5 fusion.4
  203.9 0.4 fusion.25
  204.3 39.3 %convolution_bitcast_fusion.4 = f32[4,576,16]{1,2,0:T(8,128)} fusion(f32[4,576,4608]{2,1,0:T(8,128)} %param.6, f32[16,4608]{1,0:T(8,128)S(1)} %fusion.25), kind=kOutput, calls=%fused_computation.10 | convolution fusion | flops 2038431744 | bytes 42909696 | tf_op jit(solution)/shard_map/aig,gk->aik/dot_general | solution.py:54
  243.7 23.9 %reduce-scatter.9.cloned.1.call-done = f32[1,576,16]{1,2,0:T(8,128)} async-done(((f32[4,576,16]{1,2,0:T(8,128)}), f32[1,576,16]{1,2,0:T(8,128)}) %reduce-scatter.9.cloned.1.call-update) | async-done | bytes 36880
  267.6 1.4 collective-permute-done.3
  269.1 0.8 pad_maximum_fusion.5
  269.9 1.5 collective-permute-start.4
  271.4 0.1 dynamic-slice_bitcast_fusion.1
  271.5 8.8 %all-gather.2 = f32[4,576,16]{1,2,0:T(8,128)S(1)} all-gather(f32[1,576,16]{1,2,0:T(8,128)S(1)} %dynamic-slice_bitcast_fusion.1), channel_id=1, replica_groups=mesh['row'=4,'col'=8] {'row'}, dimensions={0}, use_global_device_ids=true | all-gather | bytes 184320 | tf_op jit(solution)/shard_map/all_gather | solution.py:51
  280.4 2.5 collective-permute-start.5
  282.9 24.5 %convolution_bitcast_fusion.2 = f32[4608,16]{0,1:T(8,128)} fusion(f32[4,576,16]{1,2,0:T(8,128)S(1)} %all-gather.2, f32[4,576,4608]{2,1,0:T(8,128)} %param.6), kind=kOutput, calls=%fused_computation.8 | convolution fusion | flops 2038431744 | bytes 42909696 | tf_op jit(solution)/shard_map/aig,aik->gk/dot_general | solution.py:59
  307.5 0.1 pad_maximum_fusion.1
  307.7 0.2 reshape_reshape.7
  307.9 49.9 %all-reduce.8.cloned.1.call-done = f32[4608,16]{0,1:T(8,128)} async-done(((f32[4608,16]{0,1:T(8,128)}), f32[4608,16]{0,1:T(8,128)}) %all-reduce.8.cloned.1.call-update) | async-done | bytes 294928 | tf_op jit(solution)/shard_map/psum | solution.py:60
  357.8 1.0 add_add_fusion
  358.8 0.8 fusion.10
  359.6 16.3 %psum.31 = f32[48,48]{1,0:T(8,128)S(1)} all-reduce(f32[48,48]{1,0:T(8,128)S(1)} %fusion.10), channel_id=1, replica_groups=mesh['row'=4,'col'=8] {'row'}, use_global_device_ids=true, to_apply=%region_8.11 | all-reduce | flops 2304 | bytes 18432 | tf_op jit(solution)/shard_map/psum | solution.py:34
  375.9 0.1 slice_bitcast_fusion
  376.0 0.5 convolution_bitcast_fusion
  376.5 0.1 copy.24
  376.7 0.2 fusion.43
  376.9 0.2 fusion.44
  377.1 0.1 copy.26
  377.2 1.5 cholesky.55
  378.7 0.6 compare_reduce_fusion
  379.3 0.6 fusion.38
  380.0 1.2 custom-call.7
  381.2 0.5 fusion.1
  381.7 0.4 fusion.22
  382.2 0.7 dynamic-slice_bitcast_fusion
  382.9 0.6 pad_maximum_fusion.6
  (40 shorter events, 0.9 us)
Async XLA Ops:
  8.0 82.1 %reduce-scatter.7.cloned.1.call-start = ((), (), s32[]{:S(2)}) async-start(), calls=%async_computation.4 | async-start | bytes 204800
  24.5 105.3 %copy-start.1 = (u32[32]{0:T(128)S(1)}, u32[32]{0:T(128)}, u32[]{:S(2)}) copy-start(u32[32]{0:T(128)} %constant.54) | copy-start | bytes 388
  24.5 106.6 %copy-start = (f32[576]{0:T(1024)S(1)}, f32[576]{0:T(1024)}, u32[]{:S(2)}) copy-start(f32[576]{0:T(1024)} %param.7) | copy-start | bytes 6916
  64.6 115.7 %all-reduce.6.cloned.1.call-start = ((), (), s32[]{:S(2)}) async-start(), calls=%async_computation.2 | async-start | bytes 589824 | tf_op jit(solution)/shard_map/psum | solution.py:60
  90.1 1.4 collective-permute-start
  92.3 10.4 %collective-permute-start.1 = (f32[2,576,16]{1,2,0:T(8,128)S(1)}, f32[2,576,16]{1,2,0:T(8,128)S(1)}, u32[]{:S(2)}, u32[]{:S(2)}) collective-permute-start(f32[2,576,16]{1,2,0:T(8,128)S(1)} %get-tuple-element.8), channel_id=1, source_target_pairs={{0,2},{1,3},{2,0},{3,1},{4,6},{5,7},{6,4},{7,5},{8,10},{9,11},{10,... | collective-permute-start | bytes 221192 | tf_op jit(solution)/shard_map/ppermute | solution.py:22
  102.8 54.8 %collective-permute-start.2 = (f32[4,576,16]{1,0,2:T(4,128)S(1)}, f32[4,576,16]{1,0,2:T(4,128)S(1)}, u32[]{:S(2)}, u32[]{:S(2)}) collective-permute-start(f32[4,576,16]{1,0,2:T(4,128)S(1)} %copy.17), channel_id=1, source_target_pairs={{0,4},{1,5},{2,6},{3,7},{4,0},{5,1},{6,2},{7,3},{8,12},{9,13},{10,... | collective-permute-start | bytes 442376 | tf_op jit(solution)/shard_map/ppermute | solution.py:22
  129.8 137.9 %reduce-scatter.9.cloned.1.call-start = ((), (), s32[]{:S(2)}) async-start(), calls=%async_computation.5 | async-start | bytes 204800
  243.6 114.1 %all-reduce.8.cloned.1.call-start = ((), (), s32[]{:S(2)}) async-start(), calls=%async_computation.3 | async-start | bytes 589824 | tf_op jit(solution)/shard_map/psum | solution.py:60
  267.6 1.4 collective-permute-start.3
  269.9 10.4 %collective-permute-start.4 = (f32[2,576,16]{1,2,0:T(8,128)S(1)}, f32[2,576,16]{1,2,0:T(8,128)S(1)}, u32[]{:S(2)}, u32[]{:S(2)}) collective-permute-start(f32[2,576,16]{1,2,0:T(8,128)S(1)} %get-tuple-element.6), channel_id=1, source_target_pairs={{0,2},{1,3},{2,0},{3,1},{4,6},{5,7},{6,4},{7,5},{8,10},{9,11},{10,... | collective-permute-start | bytes 221192 | tf_op jit(solution)/shard_map/ppermute | solution.py:22
  280.4 27.1 %collective-permute-start.5 = (f32[4,576,16]{1,0,2:T(4,128)S(1)}, f32[4,576,16]{1,0,2:T(4,128)S(1)}, u32[]{:S(2)}, u32[]{:S(2)}) collective-permute-start(f32[4,576,16]{1,0,2:T(4,128)S(1)} %copy.22), channel_id=1, source_target_pairs={{0,4},{1,5},{2,6},{3,7},{4,0},{5,1},{6,2},{7,3},{8,12},{9,13},{10,... | collective-permute-start | bytes 442376 | tf_op jit(solution)/shard_map/ppermute | solution.py:22
Sparse Core Ops, SparseCore 0:
  64.7 25.2 reduce-scatter.6
  243.8 23.8 reduce-scatter.8
Sparse Core Ops, SparseCore 1:
  129.9 50.4 all-reduce.5
  307.5 50.2 all-reduce.7
